TPU v7x, 32 devices: a whole 2x2x4 slice. The times are simulated.
32 devices in a mesh: dp: 8 (over y, x, core), mp: 4 (over z).
Axes of the slice: x: 2, y: 2, z: 4, core: 2. Of those that a mesh axis runs over, the one named last changes fastest.
Arguments:
- tokens: bfloat16 [32768, 1024], P('dp', 'mp'), may hold values from -6 to 6
- cotangent: bfloat16 [32768, 1024], P('dp', 'mp'), may hold values from -6 to 6
- norm_gain: float32 [1024], P('mp'), may hold values from 0.5 to 1.5
- ema_delta: float32 [1024, 16], P('mp'), may hold values from -4 to 2
- ema_alpha: float32 [1024, 16], P('mp'), may hold values from -1.5 to 2
- ema_beta: float32 [1024, 16], P('mp'), may hold values from -4 to 4
- ema_eta: float32 [1024, 16], P('mp'), may hold values from -1.5 to 1.5
- ema_omega: float32 [1024], P('mp'), may hold values from -4 to 4
- shared_proj: bfloat16 [1024, 128], replicated, may hold values from -0.1875 to 0.1875
- query_gain: float32 [128], replicated, may hold values from -8 to 8
- query_bias: float32 [128], replicated, may hold values from -4 to 4
- key_gain: float32 [128], replicated, may hold values from -8 to 8
- value_proj: bfloat16 [1024, 2048], P(None, 'mp'), may hold values from -0.1875 to 0.1875
- gate_proj: bfloat16 [1024, 2048], P(None, 'mp'), may hold values from -0.1875 to 0.1875
- mixer_proj: bfloat16 [1024, 1024], P(None, 'mp'), may hold values from -0.1875 to 0.1875
- update_proj: bfloat16 [1024, 1024], P(None, 'mp'), may hold values from -0.1875 to 0.1875
- output_proj: bfloat16 [2048, 1024], P('mp'), may hold values from -0.5 to 0.5
- ffn_gain: float32 [1024], P('mp'), may hold values from 0.5 to 1.5
- up_proj: bfloat16 [1024, 4096], P(None, 'mp'), may hold values from -0.1875 to 0.1875
- down_proj: bfloat16 [4096, 1024], P('mp'), may hold values from -0.09375 to 0.09375
Outputs:
- layer_out: bfloat16 [32768, 1024], P('dp', 'mp')
- token_grad: bfloat16 [32768, 1024], P('dp', 'mp')
- gain_grad: float32 [1024], P('mp')
- delta_grad: float32 [1024, 16], P('mp')
- alpha_grad: float32 [1024, 16], P('mp')
- beta_grad: float32 [1024, 16], P('mp')
- eta_grad: float32 [1024, 16], P('mp')
- omega_grad: float32 [1024], P('mp')
- shared_grad: float32 [1024, 128], replicated
- query_grad: float32 [128], replicated
- bias_grad: float32 [128], replicated
- key_grad: float32 [128], replicated
- value_grad: float32 [1024, 2048], P(None, 'mp')
- gate_grad: float32 [1024, 2048], P(None, 'mp')
- mixer_grad: float32 [1024, 1024], P(None, 'mp')
- update_grad: float32 [1024, 1024], P(None, 'mp')
- output_grad: float32 [2048, 1024], P('mp')
- ffn_grad: float32 [1024], P('mp')
- up_grad: float32 [1024, 4096], P(None, 'mp')
- down_grad: float32 [4096, 1024], P('mp')
All inputs are finite; a program needn't handle non-finite values.
Results may differ from a plain program's by a relative error of at most 0.0307.
Values may be sent and summed in bfloat16 or wider, within the bound.
A program may use at most 384 MiB of HBM per device.

v0:
```python
import jax
import jax.numpy as jnp
from jax import lax
from jax.sharding import PartitionSpec as P

D = 1024
GROUP = 128
LEN = 2048
MICRO = 2
EPS = 1e-05


def matmul(left, right):
    return jnp.dot(left, right, preferred_element_type=jnp.float32)


def matmul_tn(left, right):
    return lax.dot_general(
        left, right, (((0,), (0,)), ((), ())), preferred_element_type=jnp.float32
    )


def matmul_nt(left, right):
    return lax.dot_general(
        left, right, (((1,), (1,)), ((), ())), preferred_element_type=jnp.float32
    )


def silu_slope(values):
    logistic = jax.nn.sigmoid(values)
    return logistic * (1.0 + values * (1.0 - logistic))


def norm_forward(shard, gain):
    total, power = lax.psum((jnp.sum(shard, axis=1), jnp.sum(shard * shard, axis=1)), "mp")
    mean_row = total / D
    scale = lax.rsqrt(power / D - mean_row * mean_row + EPS)
    normed = (shard - mean_row[:, None]) * scale[:, None]
    return (normed, scale, (normed * gain).astype(jnp.bfloat16))


def norm_backward(grad, normed, scale, gain):
    gain_part = jnp.sum(grad * normed, axis=0)
    scaled = grad * gain
    first, second = lax.psum((jnp.sum(scaled, axis=1), jnp.sum(scaled * normed, axis=1)), "mp")
    back = scale[:, None] * (scaled - (first / D)[:, None] - normed * (second / D)[:, None])
    return (back, gain_part)


def ema_local(signal, delta, alpha, beta, eta):
    rate = jax.nn.sigmoid(delta)
    keep_log = jnp.log(1.0 - rate * jax.nn.sigmoid(alpha))
    push = rate * beta
    width = signal.shape[1]
    blocks = signal.reshape(-1, LEN // GROUP, GROUP, width)
    offsets = jnp.arange(GROUP, dtype=jnp.float32)
    powers = jnp.exp(offsets[:, None, None] * keep_log[None])
    kernel = jnp.sum(powers * (push * eta)[None], axis=2)
    lag = jnp.arange(GROUP)[:, None] - jnp.arange(GROUP)[None, :]
    toeplitz = jnp.where((lag >= 0)[:, :, None], jnp.take(kernel, jnp.maximum(lag, 0), axis=0), 0.0)
    inner = jnp.einsum("tsc,gbsc->gbtc", toeplitz, blocks, precision=lax.Precision.HIGHEST)
    tail = jnp.exp((GROUP - 1.0 - offsets)[:, None, None] * keep_log[None]) * push[None]
    ends = jnp.einsum("gbsc,scj->bgcj", blocks, tail, precision=lax.Precision.HIGHEST)
    carry_keep = jnp.exp(GROUP * keep_log)

    def advance(state, end_now):
        return (carry_keep * state + end_now, state)

    _, starts = lax.scan(advance, jnp.zeros(ends.shape[1:], jnp.float32), ends)
    lead = jnp.exp((offsets + 1.0)[:, None, None] * keep_log[None]) * eta[None]
    outer = jnp.einsum("tcj,bgcj->gbtc", lead, starts, precision=lax.Precision.HIGHEST)
    return (inner + outer).reshape(signal.shape)


def group_scores(query, keys):
    blocks = query.shape[0] // GROUP
    query_blocks = query.reshape(blocks, GROUP, query.shape[1])
    key_blocks = keys.reshape(blocks, GROUP, keys.shape[1])
    raw = jnp.einsum("nqz,nkz->nqk", query_blocks, key_blocks, preferred_element_type=jnp.float32)
    raw = raw * query.shape[1] ** (-0.5)
    place = jnp.arange(GROUP)
    return jnp.where((place[:, None] >= place[None, :])[None], raw, -1e30)


def local(
    tokens,
    cotangent,
    norm_gain,
    ema_delta,
    ema_alpha,
    ema_beta,
    ema_eta,
    ema_omega,
    shared_proj,
    query_gain,
    query_bias,
    key_gain,
    value_proj,
    gate_proj,
    mixer_proj,
    update_proj,
    output_proj,
    ffn_gain,
    up_proj,
    down_proj,
):
    width = tokens.shape[1]
    rows_micro = tokens.shape[0] // MICRO
    shared_rows = lax.dynamic_slice_in_dim(shared_proj, lax.axis_index("mp") * width, width, 0)
    head_scale = query_gain.shape[0] ** (-0.5)
    mixer_totals_list = tuple(
        (
            jnp.zeros(item.shape, jnp.float32)
            for item in (
                norm_gain,
                ema_delta,
                ema_alpha,
                ema_beta,
                ema_eta,
                ema_omega,
                shared_proj,
                query_gain,
                query_bias,
                key_gain,
                value_proj,
                gate_proj,
                mixer_proj,
                update_proj,
                output_proj,
            )
        )
    )
    ffn_sums = tuple(
        (jnp.zeros(item.shape, jnp.float32) for item in (ffn_gain, up_proj, down_proj))
    )
    layer_rows = []
    token_rows = []
    for batch_index in range(MICRO):
        first_row = batch_index * rows_micro
        inputs = lax.slice_in_dim(tokens, first_row, first_row + rows_micro, axis=0).astype(
            jnp.float32
        )
        grad_out = lax.slice_in_dim(cotangent, first_row, first_row + rows_micro, axis=0)
        normed_one, scale_one, normed_low = norm_forward(inputs, norm_gain)
        signal = normed_low.astype(jnp.float32)
        ema_value, ema_pull = jax.vjp(ema_local, signal, ema_delta, ema_alpha, ema_beta, ema_eta)
        mix_pre = ema_value + ema_omega * signal
        mixed_low = jax.nn.silu(mix_pre).astype(jnp.bfloat16)
        normed_all, mixed_all = (
            lax.all_gather(normed_low, "mp", axis=1, tiled=True),
            lax.all_gather(mixed_low, "mp", axis=1, tiled=True),
        )
        shared_pre = matmul(mixed_all, shared_proj)
        shared = jax.nn.silu(shared_pre)
        query = (shared * query_gain + query_bias).astype(jnp.bfloat16)
        keys = (shared * key_gain).astype(jnp.bfloat16)
        value_pre = matmul(normed_all, value_proj)
        values = jax.nn.silu(value_pre).astype(jnp.bfloat16)
        gate_pre = matmul(mixed_all, gate_proj)
        gate = jax.nn.silu(gate_pre)
        scores = group_scores(query, keys)
        peak = jnp.max(scores, axis=-1, keepdims=True)
        weights = jnp.exp(scores - peak)
        weight_sum = jnp.sum(weights, axis=-1, keepdims=True)
        log_total = peak + jnp.log(weight_sum)
        probabilities = weights / weight_sum
        blocks = probabilities.shape[0]
        value_block_rows = values.reshape(blocks, GROUP, values.shape[1])
        attention_result = jnp.einsum(
            "dzc,dcs->dzs",
            probabilities.astype(jnp.bfloat16),
            value_block_rows,
            preferred_element_type=jnp.float32,
        ).reshape(rows_micro, values.shape[1])
        hidden = (gate * attention_result).astype(jnp.bfloat16)
        attn_out = lax.psum_scatter(
            matmul(hidden, output_proj).astype(jnp.bfloat16), "mp", scatter_dimension=1, tiled=True
        ).astype(jnp.float32)
        update = jax.nn.sigmoid(matmul(mixed_all, update_proj))
        act_pre = matmul(mixed_all, mixer_proj) + attn_out
        act_value = jax.nn.silu(act_pre)
        middle = update * act_value + (1.0 - update) * inputs
        normed_two, scale_two, ffn_low = norm_forward(middle, ffn_gain)
        ffn_all = lax.all_gather(ffn_low, "mp", axis=1, tiled=True)
        up_pre = matmul(ffn_all, up_proj)
        upper = jax.nn.silu(up_pre).astype(jnp.bfloat16)
        down_out = lax.psum_scatter(
            matmul(upper, down_proj).astype(jnp.bfloat16), "mp", scatter_dimension=1, tiled=True
        ).astype(jnp.float32)
        layer_rows.append((middle + down_out).astype(jnp.bfloat16))
        grad_all = lax.all_gather(grad_out, "mp", axis=1, tiled=True)
        down_part = matmul_tn(upper, grad_all)
        d_up_pre = (matmul_nt(grad_all, down_proj) * silu_slope(up_pre)).astype(jnp.bfloat16)
        up_part = matmul_tn(ffn_all, d_up_pre)
        d_ffn_in = lax.psum_scatter(
            matmul_nt(d_up_pre, up_proj).astype(jnp.bfloat16), "mp", scatter_dimension=1, tiled=True
        ).astype(jnp.float32)
        d_middle, ffn_gain_part = norm_backward(d_ffn_in, normed_two, scale_two, ffn_gain)
        d_middle = d_middle + grad_out.astype(jnp.float32)
        ffn_sums = (ffn_sums[0] + ffn_gain_part, ffn_sums[1] + up_part, ffn_sums[2] + down_part)
        if batch_index == MICRO - 1:
            ffn_reduced = ffn_sums
        d_update_pre = (d_middle * (act_value - inputs) * update * (1.0 - update)).astype(
            jnp.bfloat16
        )
        d_act_pre = (d_middle * update * silu_slope(act_pre)).astype(jnp.bfloat16)
        d_inputs = d_middle * (1.0 - update)
        mixer_part = matmul_tn(mixed_all, d_act_pre)
        update_part = matmul_tn(mixed_all, d_update_pre)
        d_act_all = lax.all_gather(d_act_pre, "mp", axis=1, tiled=True)
        output_part = matmul_tn(hidden, d_act_all)
        d_hidden = matmul_nt(d_act_all, output_proj)
        d_gate_pre = (d_hidden * attention_result * silu_slope(gate_pre)).astype(jnp.bfloat16)
        d_attended = (d_hidden * gate).astype(jnp.bfloat16)
        attention_result_blocks = d_attended.reshape(blocks, GROUP, d_attended.shape[1])
        probs_again = jnp.exp(group_scores(query, keys) - log_total)
        d_probs = lax.psum(
            jnp.einsum(
                "gas,gcs->gac",
                attention_result_blocks,
                value_block_rows,
                preferred_element_type=jnp.float32,
            ).astype(jnp.bfloat16),
            "mp",
        ).astype(jnp.float32)
        d_value = jnp.einsum(
            "uhi,uhs->uis",
            probs_again.astype(jnp.bfloat16),
            attention_result_blocks,
            preferred_element_type=jnp.float32,
        ).reshape(rows_micro, values.shape[1])
        d_value_pre = (d_value * silu_slope(value_pre)).astype(jnp.bfloat16)
        d_scores = probs_again * (d_probs - jnp.sum(probs_again * d_probs, axis=-1, keepdims=True))
        d_scores_low = d_scores.astype(jnp.bfloat16)
        query_blocks = query.reshape(blocks, GROUP, query.shape[1])
        key_blocks = keys.reshape(blocks, GROUP, keys.shape[1])
        d_query = (
            jnp.einsum(
                "nqk,nkz->nqz", d_scores_low, key_blocks, preferred_element_type=jnp.float32
            ).reshape(rows_micro, -1)
            * head_scale
        )
        d_keys = (
            jnp.einsum(
                "nqk,nqz->nkz", d_scores_low, query_blocks, preferred_element_type=jnp.float32
            ).reshape(rows_micro, -1)
            * head_scale
        )
        query_part = jnp.sum(d_query * shared, axis=0)
        bias_part = jnp.sum(d_query, axis=0)
        key_part = jnp.sum(d_keys * shared, axis=0)
        d_shared_pre = ((d_query * query_gain + d_keys * key_gain) * silu_slope(shared_pre)).astype(
            jnp.bfloat16
        )
        shared_part = matmul_tn(mixed_all, d_shared_pre)
        value_part = matmul_tn(normed_all, d_value_pre)
        gate_part = matmul_tn(mixed_all, d_gate_pre)
        mixed_terms = matmul_nt(d_gate_pre, gate_proj) + matmul_nt(d_update_pre, update_proj)
        mixed_terms = mixed_terms + matmul_nt(d_act_pre, mixer_proj)
        normed_terms = matmul_nt(d_value_pre, value_proj)
        d_mixed, d_normed = (
            lax.psum_scatter(
                mixed_terms.astype(jnp.bfloat16), "mp", scatter_dimension=1, tiled=True
            ).astype(jnp.float32),
            lax.psum_scatter(
                normed_terms.astype(jnp.bfloat16), "mp", scatter_dimension=1, tiled=True
            ).astype(jnp.float32),
        )
        d_mixed = d_mixed + matmul_nt(d_shared_pre, shared_rows)
        d_mix_pre = d_mixed * silu_slope(mix_pre)
        omega_part = jnp.sum(d_mix_pre * signal, axis=0)
        d_signal, delta_part, alpha_part, beta_part, eta_part = ema_pull(d_mix_pre)
        d_normed = d_normed + d_signal + d_mix_pre * ema_omega
        d_tokens, gain_part = norm_backward(d_normed, normed_one, scale_one, norm_gain)
        token_rows.append((d_inputs + d_tokens).astype(jnp.bfloat16))
        summand_terms = (
            gain_part,
            delta_part,
            alpha_part,
            beta_part,
            eta_part,
            omega_part,
            shared_part,
            query_part,
            bias_part,
            key_part,
            value_part,
            gate_part,
            mixer_part,
            update_part,
            output_part,
        )
        mixer_totals_list = tuple(
            (
                running_total + summand_term
                for running_total, summand_term in zip(mixer_totals_list, summand_terms)
            )
        )
    reduced = lax.psum(
        (
            mixer_totals_list[0],
            mixer_totals_list[1],
            mixer_totals_list[2],
            mixer_totals_list[3],
            mixer_totals_list[4],
            mixer_totals_list[5],
            mixer_totals_list[6],
            mixer_totals_list[7],
            mixer_totals_list[8],
            mixer_totals_list[9],
            mixer_totals_list[10],
            mixer_totals_list[11],
            mixer_totals_list[12],
            mixer_totals_list[13],
            mixer_totals_list[14],
            ffn_sums[0],
            ffn_sums[1],
            ffn_sums[2],
        ),
        "dp",
    )
    mixer_reduced = reduced[:15]
    ffn_reduced = reduced[15:]
    layer_out = jnp.concatenate(layer_rows, axis=0)
    token_grad = jnp.concatenate(token_rows, axis=0)
    return (
        layer_out,
        token_grad,
        mixer_reduced[0],
        mixer_reduced[1],
        mixer_reduced[2],
        mixer_reduced[3],
        mixer_reduced[4],
        mixer_reduced[5],
        mixer_reduced[6],
        mixer_reduced[7],
        mixer_reduced[8],
        mixer_reduced[9],
        mixer_reduced[10],
        mixer_reduced[11],
        mixer_reduced[12],
        mixer_reduced[13],
        mixer_reduced[14],
        ffn_reduced[0],
        ffn_reduced[1],
        ffn_reduced[2],
    )


def solution(mesh):
    in_specs = (
        P("dp", "mp"),
        P("dp", "mp"),
        P("mp"),
        P("mp", None),
        P("mp", None),
        P("mp", None),
        P("mp", None),
        P("mp"),
        P(),
        P(),
        P(),
        P(),
        P(None, "mp"),
        P(None, "mp"),
        P(None, "mp"),
        P(None, "mp"),
        P("mp", None),
        P("mp"),
        P(None, "mp"),
        P("mp", None),
    )
    out_specs = (
        P("dp", "mp"),
        P("dp", "mp"),
        P("mp"),
        P("mp", None),
        P("mp", None),
        P("mp", None),
        P("mp", None),
        P("mp"),
        P(),
        P(),
        P(),
        P(),
        P(None, "mp"),
        P(None, "mp"),
        P(None, "mp"),
        P(None, "mp"),
        P("mp", None),
        P("mp"),
        P(None, "mp"),
        P("mp", None),
    )
    return jax.shard_map(local, mesh=mesh, in_specs=in_specs, out_specs=out_specs, check_vma=False)
```

profile of v0, /device:TPU:0, one launch (start us, length us, event | category | flops | bytes accessed | tf_op | source)
XLA Modules:
  0.0 2425.9 jit_solution(17531408031681746158)
XLA Ops:
  15.4 21.4 all-reduce.5
  55.5 66.9 %gather_fusion = f32[16384,256]{1,0:T(8,128)} fusion(f32[128,256]{1,0:T(8,128)S(1)} %copy.189, s32[16384]{0:T(1024)} %broadcast_clamp_fusion), kind=kCustom, calls=%fused_computation.clone | custom fusion | bytes 33619968 | tf_op jit(solution)/shard_map/jvp(jit(_take))/gather | solution.py:60
  179.8 21.2 while.64
  208.5 21.2 while.65
  262.0 76.3 %all-gather.11.cloned.1.call-done = bf16[2048,1024]{1,0:T(8,128)(2,1)} async-done(((bf16[2048,256]{1,0:T(8,128)(2,1)}), bf16[2048,1024]{1,0:T(8,128)(2,1)}) %all-gather.11.cloned.1.call-update) | async-done | bytes 4194320 | tf_op jit(solution)/shard_map/all_gather | solution.py:151
  341.8 77.5 %all-gather.17.cloned.1.call-done = bf16[2048,1024]{1,0:T(8,128)(2,1)} async-done(((bf16[2048,256]{1,0:T(8,128)(2,1)}), bf16[2048,1024]{1,0:T(8,128)(2,1)}) %all-gather.17.cloned.1.call-update) | async-done | bytes 4194320 | tf_op jit(solution)/shard_map/all_gather | solution.py:151
  425.6 74.6 %all-gather.19.cloned.1.call-done = bf16[2048,1024]{1,0:T(8,128)(2,1)} async-done(((bf16[2048,256]{1,0:T(8,128)(2,1)}), bf16[2048,1024]{1,0:T(8,128)(2,1)}) %all-gather.19.cloned.1.call-update) | async-done | bytes 4194320 | tf_op jit(solution)/shard_map/all_gather | solution.py:150
  524.1 56.2 %all-gather.13.cloned.1.call-done = bf16[2048,1024]{1,0:T(8,128)(2,1)} async-done(((bf16[2048,256]{1,0:T(8,128)(2,1)}), bf16[2048,1024]{1,0:T(8,128)(2,1)}) %all-gather.13.cloned.1.call-update) | async-done | bytes 4194320 | tf_op jit(solution)/shard_map/all_gather | solution.py:150
  608.0 49.4 %reduce-scatter.15.cloned.1.call-done = bf16[2048,256]{1,0:T(8,128)(2,1)} async-done(((bf16[2048,1024]{1,0:T(8,128)(2,1)}), bf16[2048,256]{1,0:T(8,128)(2,1)}) %reduce-scatter.15.cloned.1.call-update) | async-done | bytes 1048592 | tf_op jit(solution)/shard_map/reduce_scatter | solution.py:176
  662.5 74.5 %reduce-scatter.11.cloned.1.call-done = bf16[2048,256]{1,0:T(8,128)(2,1)} async-done(((bf16[2048,1024]{1,0:T(8,128)(2,1)}), bf16[2048,256]{1,0:T(8,128)(2,1)}) %reduce-scatter.11.cloned.1.call-update) | async-done | bytes 1048592 | tf_op jit(solution)/shard_map/reduce_scatter | solution.py:176
  773.2 75.6 %all-gather.15.cloned.1.call-done = bf16[2048,1024]{1,0:T(8,128)(2,1)} async-done(((bf16[2048,256]{1,0:T(8,128)(2,1)}), bf16[2048,1024]{1,0:T(8,128)(2,1)}) %all-gather.15.cloned.1.call-update) | async-done | bytes 4194320 | tf_op jit(solution)/shard_map/all_gather | solution.py:184
  859.5 69.6 %all-gather.23.cloned.1.call-done = bf16[2048,1024]{1,0:T(8,128)(2,1)} async-done(((bf16[2048,256]{1,0:T(8,128)(2,1)}), bf16[2048,1024]{1,0:T(8,128)(2,1)}) %all-gather.23.cloned.1.call-update) | async-done | bytes 4194320 | tf_op jit(solution)/shard_map/all_gather | solution.py:191
  949.5 74.8 %reduce-scatter.19.cloned.1.call-done = bf16[2048,256]{1,0:T(8,128)(2,1)} async-done(((bf16[2048,1024]{1,0:T(8,128)(2,1)}), bf16[2048,256]{1,0:T(8,128)(2,1)}) %reduce-scatter.19.cloned.1.call-update) | async-done | bytes 1048592 | tf_op jit(solution)/shard_map/reduce_scatter | solution.py:195
  1030.0 80.4 %all-gather.21.cloned.1.call-done = bf16[2048,1024]{1,0:T(8,128)(2,1)} async-done(((bf16[2048,256]{1,0:T(8,128)(2,1)}), bf16[2048,1024]{1,0:T(8,128)(2,1)}) %all-gather.21.cloned.1.call-update) | async-done | bytes 4194320 | tf_op jit(solution)/shard_map/all_gather | solution.py:184
  1119.4 71.4 %all-gather.27.cloned.1.call-done = bf16[2048,1024]{1,0:T(8,128)(2,1)} async-done(((bf16[2048,256]{1,0:T(8,128)(2,1)}), bf16[2048,1024]{1,0:T(8,128)(2,1)}) %all-gather.27.cloned.1.call-update) | async-done | bytes 4194320 | tf_op jit(solution)/shard_map/all_gather | solution.py:191
  1211.4 74.8 %reduce-scatter.25.cloned.1.call-done = bf16[2048,256]{1,0:T(8,128)(2,1)} async-done(((bf16[2048,1024]{1,0:T(8,128)(2,1)}), bf16[2048,256]{1,0:T(8,128)(2,1)}) %reduce-scatter.25.cloned.1.call-update) | async-done | bytes 1048592 | tf_op jit(solution)/shard_map/reduce_scatter | solution.py:195
  1326.6 66.7 %all-gather.29.cloned.1.call-done = bf16[2048,1024]{1,0:T(8,128)(2,1)} async-done(((bf16[2048,256]{1,0:T(8,128)(2,1)}), bf16[2048,1024]{1,0:T(8,128)(2,1)}) %all-gather.29.cloned.1.call-update) | async-done | bytes 4194320 | tf_op jit(solution)/shard_map/all_gather | solution.py:210
  1404.4 69.1 %all-gather.25.cloned.1.call-done = bf16[2048,1024]{1,0:T(8,128)(2,1)} async-done(((bf16[2048,256]{1,0:T(8,128)(2,1)}), bf16[2048,1024]{1,0:T(8,128)(2,1)}) %all-gather.25.cloned.1.call-update) | async-done | bytes 4194320 | tf_op jit(solution)/shard_map/all_gather | solution.py:210
  1645.6 23.4 while.67
  1669.0 24.7 %reduce-scatter.23.cloned.1.call-done = bf16[2048,256]{1,0:T(8,128)(2,1)} async-done(((bf16[2048,1024]{1,0:T(8,128)(2,1)}), bf16[2048,256]{1,0:T(8,128)(2,1)}) %reduce-scatter.23.cloned.1.call-update) | async-done | bytes 1048592 | tf_op jit(solution)/shard_map/reduce_scatter | solution.py:262
  1708.6 23.4 while.66
  1823.9 99.6 %scatter_custom_fusion = f32[128,256]{1,0:T(8,128)} fusion(s32[16384]{0:T(1024)S(1)} %fusion.236, f32[16384,256]{1,0:T(8,128)} %bitcast.424, f32[]{:T(128)} %constant.164.clone.1), kind=kCustom, calls=%fused_computation.354 | custom fusion | flops 4194304 | bytes 131584 | tf_op jit(solution)/shard_map/transpose(jvp(jit(_take)))/scatter-add | solution.py:60
  1960.0 99.4 %scatter_custom_fusion.1 = f32[128,256]{1,0:T(8,128)} fusion(s32[16384]{0:T(1024)S(1)} %fusion.236, f32[16384,256]{1,0:T(8,128)} %bitcast.423, f32[]{:T(128)} %constant.164.clone.1), kind=kCustom, calls=%fused_computation.352 | custom fusion | flops 4194304 | bytes 131584 | tf_op jit(solution)/shard_map/transpose(jvp(jit(_take)))/scatter-add | solution.py:60
  2155.8 233.3 %all-reduce.13.cloned.1.call-done = (f32[1024,128]{1,0:T(8,128)}, f32[1024,512]{1,0:T(8,128)}, f32[1024,512]{1,0:T(8,128)}, f32[1024,256]{1,0:T(8,128)}, f32[102...) async-done(((f32[1024,128]{1,0:T(8,128)}, f32[1024,512]{1,0:T(8,128)}, f32[1024,512]{1,0:T(8,128)}, f32[1024,256]{1,0:T(8,128)}, ...) | async-done | bytes 17301520 | tf_op jit(solution)/shard_map/psum | solution.py:299
  (797 shorter events, 873.2 us)
Async XLA Ops:
  7.2 841.6 %copy-start = (bf16[1024,1024]{1,0:T(8,128)(2,1)S(1)}, bf16[1024,1024]{1,0:T(8,128)(2,1)}, u32[]{:S(2)}) copy-start(bf16[1024,1024]{1,0:T(8,128)(2,1)} %param.48) | copy-start | bytes 6291460
  7.3 331.0 %all-gather.11.cloned.1.call-start = ((), (), s32[]{:S(2)}) async-start(), calls=%async_computation.10 | async-start | bytes 5242880 | tf_op jit(solution)/shard_map/all_gather | solution.py:151
  259.3 159.9 %all-gather.17.cloned.1.call-start = ((), (), s32[]{:S(2)}) async-start(), calls=%async_computation.15 | async-start | bytes 5242880 | tf_op jit(solution)/shard_map/all_gather | solution.py:151
  260.1 240.0 %all-gather.19.cloned.1.call-start = ((), (), s32[]{:S(2)}) async-start(), calls=%async_computation.16 | async-start | bytes 5242880 | tf_op jit(solution)/shard_map/all_gather | solution.py:150
  260.8 319.5 %all-gather.13.cloned.1.call-start = ((), (), s32[]{:S(2)}) async-start(), calls=%async_computation.11 | async-start | bytes 5242880 | tf_op jit(solution)/shard_map/all_gather | solution.py:150
  261.4 396.0 %reduce-scatter.15.cloned.1.call-start = ((), (), s32[]{:S(2)}) async-start(), calls=%async_computation.17 | async-start | bytes 5242880 | tf_op jit(solution)/shard_map/reduce_scatter | solution.py:176
  522.0 215.0 %reduce-scatter.11.cloned.1.call-start = ((), (), s32[]{:S(2)}) async-start(), calls=%async_computation.12 | async-start | bytes 5242880 | tf_op jit(solution)/shard_map/reduce_scatter | solution.py:176
  602.2 246.6 %all-gather.15.cloned.1.call-start = ((), (), s32[]{:S(2)}) async-start(), calls=%async_computation.13 | async-start | bytes 5242880 | tf_op jit(solution)/shard_map/all_gather | solution.py:184
  769.7 159.5 %all-gather.23.cloned.1.call-start = ((), (), s32[]{:S(2)}) async-start(), calls=%async_computation.20 | async-start | bytes 5242880 | tf_op jit(solution)/shard_map/all_gather | solution.py:191
  772.7 251.6 %reduce-scatter.19.cloned.1.call-start = ((), (), s32[]{:S(2)}) async-start(), calls=%async_computation.21 | async-start | bytes 5242880 | tf_op jit(solution)/shard_map/reduce_scatter | solution.py:195
  949.3 161.1 %all-gather.21.cloned.1.call-start = ((), (), s32[]{:S(2)}) async-start(), calls=%async_computation.18 | async-start | bytes 5242880 | tf_op jit(solution)/shard_map/all_gather | solution.py:184
  1029.2 161.7 %all-gather.27.cloned.1.call-start = ((), (), s32[]{:S(2)}) async-start(), calls=%async_computation.25 | async-start | bytes 5242880 | tf_op jit(solution)/shard_map/all_gather | solution.py:191
  1029.9 256.3 %reduce-scatter.25.cloned.1.call-start = ((), (), s32[]{:S(2)}) async-start(), calls=%async_computation.26 | async-start | bytes 5242880 | tf_op jit(solution)/shard_map/reduce_scatter | solution.py:195
  1211.2 182.2 %all-gather.29.cloned.1.call-start = ((), (), s32[]{:S(2)}) async-start(), calls=%async_computation.27 | async-start | bytes 5242880 | tf_op jit(solution)/shard_map/all_gather | solution.py:210
  1314.2 159.3 %all-gather.25.cloned.1.call-start = ((), (), s32[]{:S(2)}) async-start(), calls=%async_computation.22 | async-start | bytes 5242880 | tf_op jit(solution)/shard_map/all_gather | solution.py:210
  1320.5 290.7 %all-reduce.15.cloned.1.call-start = ((), (), s32[]{:S(2)}) async-start(), calls=%async_computation.32 | async-start | bytes 2097152 | tf_op jit(solution)/shard_map/psum | solution.py:217
  1484.8 146.0 %reduce-scatter.29.cloned.1.call-start = ((), (), s32[]{:S(2)}) async-start(), calls=%async_computation.29 | async-start | bytes 5242880 | tf_op jit(solution)/shard_map/reduce_scatter | solution.py:262
  1496.7 197.0 %reduce-scatter.23.cloned.1.call-start = ((), (), s32[]{:S(2)}) async-start(), calls=%async_computation.24 | async-start | bytes 5242880 | tf_op jit(solution)/shard_map/reduce_scatter | solution.py:262
  1505.8 585.5 %reduce-scatter.27.cloned.1.call-start = ((), (), s32[]{:S(2)}) async-start(), calls=%async_computation.28 | async-start | bytes 5242880 | tf_op jit(solution)/shard_map/reduce_scatter | solution.py:265
  1517.2 574.2 %reduce-scatter.21.cloned.1.call-start = ((), (), s32[]{:S(2)}) async-start(), calls=%async_computation.23 | async-start | bytes 5242880 | tf_op jit(solution)/shard_map/reduce_scatter | solution.py:265
  1528.5 597.5 %reduce-scatter.17.cloned.1.call-start = ((), (), s32[]{:S(2)}) async-start(), calls=%async_computation.19 | async-start | bytes 5242880 | tf_op jit(solution)/shard_map/reduce_scatter | solution.py:187
  1539.5 594.2 %reduce-scatter.13.cloned.1.call-start = ((), (), s32[]{:S(2)}) async-start(), calls=%async_computation.14 | async-start | bytes 5242880 | tf_op jit(solution)/shard_map/reduce_scatter | solution.py:187
  1549.7 606.1 %all-reduce.11.cloned.1.call-start = ((), (), s32[]{:S(2)}) async-start(), calls=%async_computation.30 | async-start | bytes 140288 | tf_op jit(solution)/shard_map/psum | solution.py:299
  2102.1 286.9 %all-reduce.13.cloned.1.call-start = ((), (), s32[]{:S(2)}) async-start(), calls=%async_computation.31 | async-start | bytes 34603008 | tf_op jit(solution)/shard_map/psum | solution.py:299
  (188 other events, 4990.9 us)
Sparse Core Ops, SparseCore 0:
  259.5 78.7 all-gather.10
  340.4 78.7 all-gather.16
  421.4 78.7 all-gather.18
  501.6 78.7 all-gather.12
  582.5 74.9 reduce-scatter.14
  659.7 77.2 reduce-scatter.10
  769.8 78.9 all-gather.14
  850.4 78.7 all-gather.22
  949.4 74.9 reduce-scatter.18
  1029.3 81.0 all-gather.20
  1112.0 78.7 all-gather.26
  1211.3 74.9 reduce-scatter.24
  1314.3 78.9 all-gather.28
  1394.8 78.7 all-gather.24
  1484.9 50.3 all-reduce.14
  1537.5 76.1 reduce-scatter.28
  1616.4 77.2 reduce-scatter.22
  1696.0 77.2 reduce-scatter.26
  1776.2 77.2 reduce-scatter.20
  1855.7 77.2 reduce-scatter.16
  1935.3 77.2 reduce-scatter.12
  2102.2 53.4 all-reduce.10
  2161.5 227.5 all-reduce.12
where the time goes:
time: 2440 us; the launch traced here: 2430 us
  waiting for transfers between devices  1260 us (52%)
  matrix products  442 us (18%)
  other arithmetic  370 us (15%)
  local copies, waits for them, and re-layouts  253 us (10%)
  blocking collectives  76.4 us (3%)
    psum x2, waiting for transfers between devices, local(): lax.psum((mixer_totals_list[0], mixer_totals_list[1], mixer_totals_list[2...  246 us
    scatter-add x2, other arithmetic, ema_local(): jnp.take(kernel, jnp.maximum(lag, 0), axis=0)  199 us
    all_gather x2, waiting for transfers between devices, local(): ffn_all = lax.all_gather(ffn_low, 'mp', axis=1, tiled=True)  156 us
    all_gather x2, waiting for transfers between devices, local(): lax.all_gather(mixed_low, 'mp', axis=1, tiled=True)  154 us
    reduce_scatter x2, waiting for transfers between devices, local(): lax.psum_scatter(matmul_nt(d_up_pre, up_proj).astype(jnp.bfloat16), 'mp',...  150 us
    all_gather x2, waiting for transfers between devices, local(): grad_all = lax.all_gather(grad_out, 'mp', axis=1, tiled=True)  141 us
    all_gather x2, waiting for transfers between devices, local(): d_act_all = lax.all_gather(d_act_pre, 'mp', axis=1, tiled=True)  136 us
    all_gather x2, waiting for transfers between devices, local(): lax.all_gather(normed_low, 'mp', axis=1, tiled=True)  131 us
  transfers between devices with their start and end apart: 23, of which 17 were waited for; matrix products, arithmetic and copies ran while one was open for 29% of the time, Pallas kernels for 0%

commit v1 on v0

--- a/solution.py
+++ b/solution.py
@@ -1,3 +1,4 @@
+import functools
 import jax
 import jax.numpy as jnp
 from jax import lax
@@ -8,6 +9,34 @@
 LEN = 2048
 MICRO = 2
 EPS = 1e-05
+
+
+def rates_connect(content, axis_k):
+    mat_out, f_now, r2 = (lax.axis_size("mp"), lax.axis_index("mp"), content.shape[axis_k])
+    seen = tuple(((ii, (ii + 1) % mat_out) for ii in range(mat_out)))
+    rows = tuple(((ii, (ii - 1) % mat_out) for ii in range(mat_out)))
+    then = jnp.zeros(
+        (*content.shape[:axis_k], mat_out * r2, *content.shape[axis_k + 1 :]), content.dtype
+    )
+    then = lax.dynamic_update_slice_in_dim(then, content, f_now * r2, axis=axis_k)
+    formed = piece_out = content
+    earlier = mat_out // 2
+    j0 = 1
+    while j0 < earlier + 1:
+        formed = lax.ppermute(formed, "mp", seen)
+        then = lax.dynamic_update_slice_in_dim(
+            then, formed, (f_now - j0) % mat_out * r2, axis=axis_k
+        )
+        if j0 < mat_out - earlier:
+            piece_out = lax.ppermute(piece_out, "mp", rows)
+            then = lax.dynamic_update_slice_in_dim(
+                then, piece_out, (f_now + j0) % mat_out * r2, axis=axis_k
+            )
+        j0 += 1
+    return then
+
+
+compute_the_quotas = functools.partial(rates_connect, axis_k=1)
 
 
 def matmul(left, right):
@@ -148,7 +177,7 @@
         mixed_low = jax.nn.silu(mix_pre).astype(jnp.bfloat16)
         normed_all, mixed_all = (
             lax.all_gather(normed_low, "mp", axis=1, tiled=True),
-            lax.all_gather(mixed_low, "mp", axis=1, tiled=True),
+            compute_the_quotas(mixed_low),
         )
         shared_pre = matmul(mixed_all, shared_proj)
         shared = jax.nn.silu(shared_pre)

time: 2440 us -> 2340 us (0.959)
  waiting for transfers between devices: 1260 us -> 1100 us
  starting transfers between devices: 3.57 us -> 55.8 us
    all_gather x2 -> x0, waiting for transfers between devices: 154 us -> none  [local(): lax.all_gather(mixed_low, 'mp', axis=1, tiled=True)]
    ppermute x0 -> x6, waiting for transfers between devices: none -> 134 us  [the longest x4 81.9 us: rates_connect(): formed = lax.ppermute(formed, 'mp', seen)]
    all_gather x2, waiting for transfers between devices: 131 us -> 0.04 us  [local(): lax.all_gather(normed_low, 'mp', axis=1, tiled=True)]
    ppermute x0 -> x6, starting transfers between devices: none -> 52.3 us  [the longest x4 47.5 us: rates_connect(): formed = lax.ppermute(formed, 'mp', seen)]
    unnamed x401 -> x393, local copies, waits for them, and re-layouts: 75.8 us -> 70.7 us
  transfers between devices with their start and end apart: 23 -> 27, of which waited for: 17 -> 18; matrix products, arithmetic and copies ran while one was open for 29% -> 40% of each run, Pallas kernels for 0% -> 0%
where the time goes in v1:
time: 2340 us; the launch traced here: 2320 us
  waiting for transfers between devices  1100 us (47%)
  matrix products  452 us (19%)
  other arithmetic  360 us (15%)
  local copies, waits for them, and re-layouts  265 us (11%)
  blocking collectives  75.2 us (3%)
  starting transfers between devices  55.8 us (2%)
    psum x2, waiting for transfers between devices, local(): lax.psum((mixer_totals_list[0], mixer_totals_list[1], mixer_totals_list[2...  246 us
    scatter-add x2, other arithmetic, ema_local(): jnp.take(kernel, jnp.maximum(lag, 0), axis=0)  199 us
    all_gather x2, waiting for transfers between devices, local(): ffn_all = lax.all_gather(ffn_low, 'mp', axis=1, tiled=True)  156 us
    reduce_scatter x2, waiting for transfers between devices, local(): lax.psum_scatter(matmul_nt(d_up_pre, up_proj).astype(jnp.bfloat16), 'mp',...  150 us
    all_gather x2, waiting for transfers between devices, local(): grad_all = lax.all_gather(grad_out, 'mp', axis=1, tiled=True)  141 us
    all_gather x2, waiting for transfers between devices, local(): d_act_all = lax.all_gather(d_act_pre, 'mp', axis=1, tiled=True)  136 us
    reduce_scatter x2, waiting for transfers between devices, local(): lax.psum_scatter(matmul(hidden, output_proj).astype(jnp.bfloat16), 'mp',...  117 us
    dot_general x16, matrix products, matmul(): return jnp.dot(left, right, preferred_element_type=jnp.float32)  106 us
  transfers between devices with their start and end apart: 27, of which 18 were waited for; matrix products, arithmetic and copies ran while one was open for 40% of the time, Pallas kernels for 0%

profile of v1, /device:TPU:0, one launch (start us, length us, event | category | flops | bytes accessed | tf_op | source)
XLA Modules:
  0.0 2324.9 jit_solution(11035230540819310518)
XLA Ops:
  10.1 20.8 all-reduce.5
  51.1 21.2 while.64
  82.2 21.2 while.65
  116.3 67.0 %gather_fusion = f32[16384,256]{1,0:T(8,128)} fusion(f32[128,256]{1,0:T(8,128)S(1)} %copy.189, s32[16384]{0:T(1024)} %broadcast_clamp_fusion), kind=kCustom, calls=%fused_computation.clone | custom fusion | bytes 33619968 | tf_op jit(solution)/shard_map/jvp(jit(_take))/gather | solution.py:89
  267.7 24.5 %collective-permute-done.3 = bf16[2048,256]{1,0:T(8,128)(2,1)} collective-permute-done((bf16[2048,256]{1,0:T(8,128)(2,1)S(1)}, bf16[2048,256]{1,0:T(8,128)(2,1)}, u32[]{:S(2)}, u32[]{:S(2)}) %collective-permute-start.3) | collective-permute-done | bytes 1048608 | tf_op jit(solution)/shard_map/ppermute | solution.py:26
  298.5 38.5 %collective-permute-done = bf16[2048,256]{1,0:T(8,128)(2,1)} collective-permute-done((bf16[2048,256]{1,0:T(8,128)(2,1)}, bf16[2048,256]{1,0:T(8,128)(2,1)}, u32[]{:S(2)}, u32[]{:S(2)}) %collective-permute-start) | collective-permute-done | bytes 1048608 | tf_op jit(solution)/shard_map/ppermute | solution.py:26
  337.0 40.7 %collective-permute-start.2 = (bf16[2048,256]{1,0:T(8,128)(2,1)}, bf16[2048,256]{1,0:T(8,128)(2,1)S(1)}, u32[]{:S(2)}, u32[]{:S(2)}) collective-permute-start(bf16[2048,256]{1,0:T(8,128)(2,1)} %collective-permute-done), channel_id=1, source_target_pairs={{0,1},{1,2},{2,3},{3,0},{4,5},{5,6},{6,7},{7,4},{8,9},{9,10},{10,1... | collective-permute-start | bytes 3145736 | tf_op jit(solution)/shard_map/ppermute | solution.py:26
  384.6 51.9 %collective-permute-done.1 = bf16[2048,256]{1,0:T(8,128)(2,1)} collective-permute-done((bf16[2048,256]{1,0:T(8,128)(2,1)}, bf16[2048,256]{1,0:T(8,128)(2,1)}, u32[]{:S(2)}, u32[]{:S(2)}) %collective-permute-start.1) | collective-permute-done | bytes 1048608 | tf_op jit(solution)/shard_map/ppermute | solution.py:31
  523.5 42.3 %reduce-scatter.15.cloned.1.call-done = bf16[2048,256]{1,0:T(8,128)(2,1)} async-done(((bf16[2048,1024]{1,0:T(8,128)(2,1)}), bf16[2048,256]{1,0:T(8,128)(2,1)}) %reduce-scatter.15.cloned.1.call-update) | async-done | bytes 1048592 | tf_op jit(solution)/shard_map/reduce_scatter | solution.py:205
  570.9 74.5 %reduce-scatter.11.cloned.1.call-done = bf16[2048,256]{1,0:T(8,128)(2,1)} async-done(((bf16[2048,1024]{1,0:T(8,128)(2,1)}), bf16[2048,256]{1,0:T(8,128)(2,1)}) %reduce-scatter.11.cloned.1.call-update) | async-done | bytes 1048592 | tf_op jit(solution)/shard_map/reduce_scatter | solution.py:205
  658.1 18.2 all-reduce.4
  682.7 75.6 %all-gather.11.cloned.1.call-done = bf16[2048,1024]{1,0:T(8,128)(2,1)} async-done(((bf16[2048,256]{1,0:T(8,128)(2,1)}), bf16[2048,1024]{1,0:T(8,128)(2,1)}) %all-gather.11.cloned.1.call-update) | async-done | bytes 4194320 | tf_op jit(solution)/shard_map/all_gather | solution.py:213
  769.0 69.4 %all-gather.17.cloned.1.call-done = bf16[2048,1024]{1,0:T(8,128)(2,1)} async-done(((bf16[2048,256]{1,0:T(8,128)(2,1)}), bf16[2048,1024]{1,0:T(8,128)(2,1)}) %all-gather.17.cloned.1.call-update) | async-done | bytes 4194320 | tf_op jit(solution)/shard_map/all_gather | solution.py:220
  858.8 74.8 %reduce-scatter.19.cloned.1.call-done = bf16[2048,256]{1,0:T(8,128)(2,1)} async-done(((bf16[2048,1024]{1,0:T(8,128)(2,1)}), bf16[2048,256]{1,0:T(8,128)(2,1)}) %reduce-scatter.19.cloned.1.call-update) | async-done | bytes 1048592 | tf_op jit(solution)/shard_map/reduce_scatter | solution.py:224
  939.3 80.4 %all-gather.15.cloned.1.call-done = bf16[2048,1024]{1,0:T(8,128)(2,1)} async-done(((bf16[2048,256]{1,0:T(8,128)(2,1)}), bf16[2048,1024]{1,0:T(8,128)(2,1)}) %all-gather.15.cloned.1.call-update) | async-done | bytes 4194320 | tf_op jit(solution)/shard_map/all_gather | solution.py:213
  1028.8 71.4 %all-gather.21.cloned.1.call-done = bf16[2048,1024]{1,0:T(8,128)(2,1)} async-done(((bf16[2048,256]{1,0:T(8,128)(2,1)}), bf16[2048,1024]{1,0:T(8,128)(2,1)}) %all-gather.21.cloned.1.call-update) | async-done | bytes 4194320 | tf_op jit(solution)/shard_map/all_gather | solution.py:220
  1120.6 74.8 %reduce-scatter.25.cloned.1.call-done = bf16[2048,256]{1,0:T(8,128)(2,1)} async-done(((bf16[2048,1024]{1,0:T(8,128)(2,1)}), bf16[2048,256]{1,0:T(8,128)(2,1)}) %reduce-scatter.25.cloned.1.call-update) | async-done | bytes 1048592 | tf_op jit(solution)/shard_map/reduce_scatter | solution.py:224
  1235.9 66.7 %all-gather.23.cloned.1.call-done = bf16[2048,1024]{1,0:T(8,128)(2,1)} async-done(((bf16[2048,256]{1,0:T(8,128)(2,1)}), bf16[2048,1024]{1,0:T(8,128)(2,1)}) %all-gather.23.cloned.1.call-update) | async-done | bytes 4194320 | tf_op jit(solution)/shard_map/all_gather | solution.py:239
  1313.6 69.1 %all-gather.19.cloned.1.call-done = bf16[2048,1024]{1,0:T(8,128)(2,1)} async-done(((bf16[2048,256]{1,0:T(8,128)(2,1)}), bf16[2048,1024]{1,0:T(8,128)(2,1)}) %all-gather.19.cloned.1.call-update) | async-done | bytes 4194320 | tf_op jit(solution)/shard_map/all_gather | solution.py:239
  1559.2 23.4 %while.66 = (s32[]{:T(128)}, f32[256,16]{0,1:T(8,128)S(1)}, f32[1,256,16]{1,2,0:T(8,128)S(1)}, f32[16,1,256,16]{2,3,1,0:T(8,128)S(1)}, f32[16,1,256,16]{2,3,1,0:...) while((s32[]{:T(128)}, f32[256,16]{0,1:T(8,128)S(1)}, ...), condition=%wide.region_39.41_spmd.clone, body=%wide.region_38.40_spmd.clone.sunk | while | flops 32772 | bytes 165516 | solution.py:98
  1582.6 19.6 reduce-scatter.29.cloned.1.call-done
  1722.7 99.6 %scatter_custom_fusion = f32[128,256]{1,0:T(8,128)} fusion(s32[16384]{0:T(1024)S(1)} %fusion.236, f32[16384,256]{1,0:T(8,128)} %bitcast.422, f32[]{:T(128)} %constant.194.clone.1), kind=kCustom, calls=%fused_computation.354 | custom fusion | flops 4194304 | bytes 131584 | tf_op jit(solution)/shard_map/transpose(jvp(jit(_take)))/scatter-add | solution.py:89
  1858.7 99.4 %scatter_custom_fusion.1 = f32[128,256]{1,0:T(8,128)} fusion(s32[16384]{0:T(1024)S(1)} %fusion.236, f32[16384,256]{1,0:T(8,128)} %bitcast.421, f32[]{:T(128)} %constant.194.clone.1), kind=kCustom, calls=%fused_computation.352 | custom fusion | flops 4194304 | bytes 131584 | tf_op jit(solution)/shard_map/transpose(jvp(jit(_take)))/scatter-add | solution.py:89
  2054.5 233.3 %all-reduce.13.cloned.1.call-done = (f32[1024,128]{1,0:T(8,128)}, f32[1024,512]{1,0:T(8,128)}, f32[1024,512]{1,0:T(8,128)}, f32[1024,256]{1,0:T(8,128)}, f32[102...) async-done(((f32[1024,128]{1,0:T(8,128)}, f32[1024,512]{1,0:T(8,128)}, f32[1024,512]{1,0:T(8,128)}, f32[1024,256]{1,0:T(8,128)}, ...) | async-done | bytes 17301520 | tf_op jit(solution)/shard_map/psum | solution.py:328
  (805 shorter events, 907.7 us)
Async XLA Ops:
  7.2 461.6 %all-gather.13.cloned.1.call-start = ((), (), s32[]{:S(2)}) async-start(), calls=%async_computation.14 | async-start | bytes 5242880 | tf_op jit(solution)/shard_map/all_gather | solution.py:179
  35.2 457.7 %all-gather.9.cloned.1.call-start = ((), (), s32[]{:S(2)}) async-start(), calls=%async_computation.10 | async-start | bytes 5242880 | tf_op jit(solution)/shard_map/all_gather | solution.py:179
  266.2 299.6 %reduce-scatter.15.cloned.1.call-start = ((), (), s32[]{:S(2)}) async-start(), calls=%async_computation.15 | async-start | bytes 5242880 | tf_op jit(solution)/shard_map/reduce_scatter | solution.py:205
  266.2 170.2 %collective-permute-start.1 = (bf16[2048,256]{1,0:T(8,128)(2,1)}, bf16[2048,256]{1,0:T(8,128)(2,1)}, u32[]{:S(2)}, u32[]{:S(2)}) collective-permute-start(bf16[2048,256]{1,0:T(8,128)(2,1)} %get-tuple-element.709), channel_id=1, source_target_pairs={{0,3},{1,0},{2,1},{3,2},{4,7},{5,4},{6,5},{7,6},{8,11},{9,8},{10,9... | collective-permute-start | bytes 3145736 | tf_op jit(solution)/shard_map/ppermute | solution.py:31
  292.1 150.5 %collective-permute-start.5 = (bf16[2048,256]{1,0:T(8,128)(2,1)}, bf16[2048,256]{1,0:T(8,128)(2,1)}, u32[]{:S(2)}, u32[]{:S(2)}) collective-permute-start(bf16[2048,256]{1,0:T(8,128)(2,1)} %collective-permute-done.3), channel_id=1, source_target_pairs={{0,1},{1,2},{2,3},{3,0},{4,5},{5,6},{6,7},{7,4},{8,9},{9,10},{10,1... | collective-permute-start | bytes 3145736 | tf_op jit(solution)/shard_map/ppermute | solution.py:26
  337.0 122.8 %collective-permute-start.2 = (bf16[2048,256]{1,0:T(8,128)(2,1)}, bf16[2048,256]{1,0:T(8,128)(2,1)S(1)}, u32[]{:S(2)}, u32[]{:S(2)}) collective-permute-start(bf16[2048,256]{1,0:T(8,128)(2,1)} %collective-permute-done), channel_id=1, source_target_pairs={{0,1},{1,2},{2,3},{3,0},{4,5},{5,6},{6,7},{7,4},{8,9},{9,10},{10,1... | collective-permute-start | bytes 3145736 | tf_op jit(solution)/shard_map/ppermute | solution.py:26
  490.7 154.7 %reduce-scatter.11.cloned.1.call-start = ((), (), s32[]{:S(2)}) async-start(), calls=%async_computation.11 | async-start | bytes 5242880 | tf_op jit(solution)/shard_map/reduce_scatter | solution.py:205
  517.8 240.5 %all-gather.11.cloned.1.call-start = ((), (), s32[]{:S(2)}) async-start(), calls=%async_computation.12 | async-start | bytes 5242880 | tf_op jit(solution)/shard_map/all_gather | solution.py:213
  679.2 159.3 %all-gather.17.cloned.1.call-start = ((), (), s32[]{:S(2)}) async-start(), calls=%async_computation.18 | async-start | bytes 5242880 | tf_op jit(solution)/shard_map/all_gather | solution.py:220
  682.2 251.4 %reduce-scatter.19.cloned.1.call-start = ((), (), s32[]{:S(2)}) async-start(), calls=%async_computation.19 | async-start | bytes 5242880 | tf_op jit(solution)/shard_map/reduce_scatter | solution.py:224
  858.6 161.2 %all-gather.15.cloned.1.call-start = ((), (), s32[]{:S(2)}) async-start(), calls=%async_computation.16 | async-start | bytes 5242880 | tf_op jit(solution)/shard_map/all_gather | solution.py:213
  938.5 161.7 %all-gather.21.cloned.1.call-start = ((), (), s32[]{:S(2)}) async-start(), calls=%async_computation.23 | async-start | bytes 5242880 | tf_op jit(solution)/shard_map/all_gather | solution.py:220
  939.2 256.2 %reduce-scatter.25.cloned.1.call-start = ((), (), s32[]{:S(2)}) async-start(), calls=%async_computation.24 | async-start | bytes 5242880 | tf_op jit(solution)/shard_map/reduce_scatter | solution.py:224
  1120.4 182.2 %all-gather.23.cloned.1.call-start = ((), (), s32[]{:S(2)}) async-start(), calls=%async_computation.25 | async-start | bytes 5242880 | tf_op jit(solution)/shard_map/all_gather | solution.py:239
  1223.4 159.3 %all-gather.19.cloned.1.call-start = ((), (), s32[]{:S(2)}) async-start(), calls=%async_computation.20 | async-start | bytes 5242880 | tf_op jit(solution)/shard_map/all_gather | solution.py:239
  1229.7 294.8 %all-reduce.15.cloned.1.call-start = ((), (), s32[]{:S(2)}) async-start(), calls=%async_computation.30 | async-start | bytes 2097152 | tf_op jit(solution)/shard_map/psum | solution.py:246
  1393.9 150.6 %reduce-scatter.23.cloned.1.call-start = ((), (), s32[]{:S(2)}) async-start(), calls=%async_computation.22 | async-start | bytes 5242880 | tf_op jit(solution)/shard_map/reduce_scatter | solution.py:291
  1405.6 196.7 %reduce-scatter.29.cloned.1.call-start = ((), (), s32[]{:S(2)}) async-start(), calls=%async_computation.27 | async-start | bytes 5242880 | tf_op jit(solution)/shard_map/reduce_scatter | solution.py:291
  1414.7 575.5 %reduce-scatter.27.cloned.1.call-start = ((), (), s32[]{:S(2)}) async-start(), calls=%async_computation.26 | async-start | bytes 5242880 | tf_op jit(solution)/shard_map/reduce_scatter | solution.py:294
  1426.1 564.2 %reduce-scatter.21.cloned.1.call-start = ((), (), s32[]{:S(2)}) async-start(), calls=%async_computation.21 | async-start | bytes 5242880 | tf_op jit(solution)/shard_map/reduce_scatter | solution.py:294
  1437.4 586.9 %reduce-scatter.17.cloned.1.call-start = ((), (), s32[]{:S(2)}) async-start(), calls=%async_computation.17 | async-start | bytes 5242880 | tf_op jit(solution)/shard_map/reduce_scatter | solution.py:216
  1448.3 583.7 %reduce-scatter.13.cloned.1.call-start = ((), (), s32[]{:S(2)}) async-start(), calls=%async_computation.13 | async-start | bytes 5242880 | tf_op jit(solution)/shard_map/reduce_scatter | solution.py:216
  1458.4 596.2 %all-reduce.11.cloned.1.call-start = ((), (), s32[]{:S(2)}) async-start(), calls=%async_computation.28 | async-start | bytes 140288 | tf_op jit(solution)/shard_map/psum | solution.py:328
  2001.0 286.8 %all-reduce.13.cloned.1.call-start = ((), (), s32[]{:S(2)}) async-start(), calls=%async_computation.29 | async-start | bytes 34603008 | tf_op jit(solution)/shard_map/psum | solution.py:328
  (188 other events, 4835.6 us)
Sparse Core Ops, SparseCore 0:
  35.3 78.7 all-gather.12
  266.3 155.6 all-gather.8
  490.8 74.9 reduce-scatter.14
  568.1 77.2 reduce-scatter.10
  679.3 78.9 all-gather.10
  759.7 78.7 all-gather.16
  858.7 74.9 reduce-scatter.18
  938.6 81.0 all-gather.14
  1021.4 78.7 all-gather.20
  1120.5 74.9 reduce-scatter.24
  1223.6 78.9 all-gather.22
  1304.0 78.7 all-gather.18
  1394.0 50.3 all-reduce.14
  1446.7 76.1 reduce-scatter.22
  1525.0 77.2 reduce-scatter.28
  1604.5 77.2 reduce-scatter.26
  1684.5 77.2 reduce-scatter.20
  1764.1 77.2 reduce-scatter.16
  1843.7 77.2 reduce-scatter.12
  2001.1 53.3 all-reduce.10
  2060.2 227.5 all-reduce.12
